TPU v7x, 256 devices: a whole 4x4x8 slice. The times are simulated.
256 devices in a mesh: grp: 16 (over z, core), ing: 16 (over y, x).
Axes of the slice: x: 4, y: 4, z: 8, core: 2. Of those that a mesh axis runs over, the one named last changes fastest.
Arguments:
- amplitudes: bfloat16 [512, 800, 800], P('grp', 'ing'), may hold values from -6 to 6
- integrals: bfloat16 [512, 800, 800], P('grp', 'ing'), may hold values from -0.0024414062 to 0.0024414062
- fock_block: bfloat16 [800, 800], P('ing'), may hold values from -0.625 to 0.625
- virtual_irrep: int32 [800], replicated, may hold values from 0 to 7, as said below
- pair_irrep: int32 [512], P(('grp', 'ing')), may hold values from 0 to 7
- pair_energy: float32 [512], P(('grp', 'ing')), may hold values from -4 to -1
- virtual_energy: float32 [800], replicated, may hold values from 0.5 to 4
Outputs:
- update: float32 [512, 800, 800], P('grp', 'ing')
Inputs may be any that keep to these rules, and one draw needn't show every extreme that they name: `virtual_irrep`: the orbitals of one irreducible representation form one contiguous run of 100 plus or minus at most 25 orbitals, and all 8 representations occur.
All inputs are finite; a program needn't handle non-finite values.
Results may differ from a plain program's by a relative error of at most 0.0029.
Values may be sent and summed in bfloat16 or wider, within the bound.
A program may use at most 128 MiB of HBM per device.

v0:
```python
import jax
import jax.numpy as jnp
from jax import lax
from jax.sharding import PartitionSpec as P


def symmetry_mask(values, pair_irrep, virtual_irrep):
    allowed = (
        jnp.bitwise_xor(virtual_irrep[:, None], virtual_irrep[None, :])[None]
        == pair_irrep[:, None, None]
    )
    return jnp.where(allowed, values, jnp.zeros_like(values))


def body(amplitudes, integrals, fock_block, virtual_irrep, pair_irrep, pair_energy, virtual_energy):
    same_irrep = virtual_irrep[:, None] == virtual_irrep[None, :]
    whole_amps, whole_ints = (
        lax.all_to_all(amplitudes, "ing", split_axis=0, concat_axis=1, tiled=True),
        lax.all_to_all(integrals, "ing", split_axis=0, concat_axis=1, tiled=True),
    )
    amp_masked = symmetry_mask(whole_amps, pair_irrep, virtual_irrep)
    int_masked = symmetry_mask(whole_ints, pair_irrep, virtual_irrep)
    partial_value = jnp.einsum(
        "paf,pef->ae", amp_masked, int_masked, preferred_element_type=jnp.float32
    )
    correction = lax.psum(partial_value, ("grp", "ing"))
    fock_full = lax.all_gather(fock_block, "ing", axis=0, tiled=True)
    fock_part = jnp.where(
        same_irrep, fock_full.astype(jnp.float32), jnp.zeros(fock_full.shape, jnp.float32)
    )
    operator_vv = (fock_part + correction).astype(jnp.bfloat16)
    product = jnp.einsum("pae,be->pab", amp_masked, operator_vv, preferred_element_type=jnp.float32)
    denominator = (
        pair_energy[:, None, None] - virtual_energy[None, :, None] - virtual_energy[None, None, :]
    )
    scaled = (product - jnp.swapaxes(product, 1, 2)) / denominator
    return lax.all_to_all(scaled, "ing", split_axis=1, concat_axis=0, tiled=True)


def solution(mesh):
    in_specs = (
        P("grp", "ing", None),
        P("grp", "ing", None),
        P("ing", None),
        P(),
        P(("grp", "ing")),
        P(("grp", "ing")),
        P(),
    )
    out_specs = P("grp", "ing", None)
    return jax.shard_map(body, mesh=mesh, in_specs=in_specs, out_specs=out_specs, check_vma=False)
```

profile of v0, /device:TPU:99, one launch (start us, length us, event | category | flops | bytes accessed | tf_op | source)
XLA Modules:
  0.0 516.4 jit_solution(2653213600742417975)
XLA Ops:
  7.4 4.4 copy.25
  11.8 6.9 %all-to-all-start = ((bf16[32,50,800]{2,1,0:T(8,128)(2,1)}), bf16[32,50,800]{2,1,0:T(8,128)(2,1)S(1)}, u32[]{:S(2)}, u32[]{:S(2)}) async-start(bf16[32,50,800]{2,1,0:T(8,128)(2,1)} %copy.25), calls=%async_computation | async-start | bytes 6422528 | tf_op jit(solution)/shard_map/all_to_all | solution.py:18
  18.7 4.5 copy.27
  23.2 0.0 copy-start.2
  23.2 39.1 %all-to-all-done = bf16[32,50,800]{2,1,0:T(8,128)(2,1)S(1)} async-done(((bf16[32,50,800]{2,1,0:T(8,128)(2,1)}), bf16[32,50,800]{2,1,0:T(8,128)(2,1)S(1)}, u32[]{:S(2)}, u32[]{:S(2)}) %all-to-all-start) | async-done | bytes 2560032 | tf_op jit(solution)/shard_map/all_to_all | solution.py:18
  62.3 8.3 %all-to-all-start.1 = ((bf16[32,50,800]{2,1,0:T(8,128)(2,1)}), bf16[32,50,800]{2,1,0:T(8,128)(2,1)}, u32[]{:S(2)}, u32[]{:S(2)}) async-start(bf16[32,50,800]{2,1,0:T(8,128)(2,1)} %copy.27), calls=%async_computation.1 | async-start | bytes 6422528 | tf_op jit(solution)/shard_map/all_to_all | solution.py:19
  70.7 0.0 all-gather.3.cloned.1.call-start
  70.7 0.7 all-gather.3.cloned.1.call-update
  71.4 0.0 all-reduce.2.cloned.1.call-start
  71.4 0.0 copy-done.2
  71.5 1.8 broadcast_xor_fusion
  73.3 3.8 copy.26
  77.1 35.5 %all-to-all-done.1 = bf16[32,50,800]{2,1,0:T(8,128)(2,1)} async-done(((bf16[32,50,800]{2,1,0:T(8,128)(2,1)}), bf16[32,50,800]{2,1,0:T(8,128)(2,1)}, u32[]{:S(2)}, u32[]{:S(2)}) %all-to-all-start.1) | async-done | bytes 2560032 | tf_op jit(solution)/shard_map/all_to_all | solution.py:19
  112.6 0.0 copy-start
  112.6 0.0 copy-start.1
  112.6 0.0 copy-start.4
  112.6 4.3 copy.28
  116.9 0.0 copy-done
  116.9 0.0 copy-done.1
  116.9 0.0 copy-done.4
  116.9 7.2 %compare_select_fusion = (bf16[2,800,800]{2,0,1:T(2,128)(2,1)S(1)}, bf16[2,800,800]{2,0,1:T(2,128)(2,1)S(1)}) fusion(bf16[16,2,50,800]{3,1,2,0:T(2,128)(2,1)S(1)} %copy.28, s32[800,800]{1,0:T(8,128)S(1)} %copy-done, s32[2]{0:T(128)S(1)} %copy-done.4, bf16[16,2,50,800]{3,1,2,0:T(2,128)(2,1)S(1)} %copy-done.1), kind=kLoop, calls=%fused_computation | loop fusion | flops 3840000 | bytes 12800008 | tf_op jit(solution)/shard_map/jit(_where)/select_n | solution.py:12
  124.1 4.8 fusion.6
  129.0 0.0 copy-start.3
  129.0 0.0 copy-start.5
  129.0 0.0 all-reduce.2.cloned.1.call-update
  129.0 0.7 copy-done.3
  129.7 0.0 copy-done.5
  129.7 0.1 broadcast_subtract_fusion
  129.7 9.6 %all-gather.3.cloned.1.call-done = bf16[16,50,800]{2,1,0:T(8,128)(2,1)} async-done(((bf16[1,50,800]{2,1,0:T(8,128)(2,1)}), bf16[16,50,800]{2,1,0:T(8,128)(2,1)}) %all-gather.3.cloned.1.call-update) | async-done | bytes 1280016 | tf_op jit(solution)/shard_map/all_gather | solution.py:27
  139.3 3.0 reshape.63
  142.4 254.5 %all-reduce.2.cloned.1.call-done = f32[800,800]{1,0:T(8,128)} async-done(((f32[800,800]{1,0:T(8,128)}), f32[800,800]{1,0:T(8,128)}) %all-reduce.2.cloned.1.call-update) | async-done | bytes 2560016 | tf_op jit(solution)/shard_map/psum | solution.py:26
  396.8 8.1 %fusion.4 = f32[2,800,800]{2,1,0:T(8,128)} fusion(bf16[2,800,800]{2,0,1:T(2,128)(2,1)S(1)} %get-tuple-element.6, f32[800,800]{1,0:T(8,128)} %all-reduce.2.cloned.1.call-done, f32[800,800]{1,0:T(8,128)} %reshape.63, s32[800]{0:T(1024)S(1)} %copy-done.2), kind=kOutput, calls=%fused_computation.8 | convolution fusion | flops 2050560000 | bytes 12803200 | tf_op jit(solution)/shard_map/pae,be->pab/dot_general | solution.py:32
  404.9 7.1 %copy.32 = f32[2,800,800]{1,2,0:T(8,128)} copy(f32[2,800,800]{2,1,0:T(8,128)} %fusion.4) | data formatting | bytes 10240000 | tf_op jit(solution)/shard_map/pae,be->pab/dot_general | solution.py:32
  412.0 5.1 fusion
  417.1 4.4 copy.33
  421.5 73.9 %all_to_all.54 = f32[2,800,800]{2,0,1:T(2,128)S(1)} all-to-all(f32[2,800,800]{2,0,1:T(2,128)S(1)} %copy.33), channel_id=1, replica_groups=mesh['grp'=16,'ing'=16] {'ing'}, dimensions={1} | all-to-all | bytes 10240000 | tf_op jit(solution)/shard_map/all_to_all | solution.py:37
  495.4 5.7 %copy.34 = f32[16,2,50,800]{3,1,0,2:T(2,128)} copy(f32[16,2,50,800]{3,1,2,0:T(2,128)S(1)} %bitcast.25) | data formatting | bytes 10240000 | tf_op jit(solution)/shard_map/all_to_all | solution.py:37
  501.1 7.8 %all_to_all.50 = f32[32,50,800]{2,0,1:T(8,128)} reshape(f32[16,2,50,800]{3,1,0,2:T(2,128)} %copy.34) | data formatting | bytes 10240000 | tf_op jit(solution)/shard_map/all_to_all | solution.py:37
Async XLA Ops:
  11.8 50.5 %all-to-all-start = ((bf16[32,50,800]{2,1,0:T(8,128)(2,1)}), bf16[32,50,800]{2,1,0:T(8,128)(2,1)S(1)}, u32[]{:S(2)}, u32[]{:S(2)}) async-start(bf16[32,50,800]{2,1,0:T(8,128)(2,1)} %copy.25), calls=%async_computation | async-start | bytes 6422528 | tf_op jit(solution)/shard_map/all_to_all | solution.py:18
  23.2 48.2 %copy-start.2 = (s32[800]{0:T(1024)S(1)}, s32[800]{0:T(1024)}, u32[]{:S(2)}) copy-start(s32[800]{0:T(1024)} %param.10) | copy-start | bytes 9604
  62.3 50.3 %all-to-all-start.1 = ((bf16[32,50,800]{2,1,0:T(8,128)(2,1)}), bf16[32,50,800]{2,1,0:T(8,128)(2,1)}, u32[]{:S(2)}, u32[]{:S(2)}) async-start(bf16[32,50,800]{2,1,0:T(8,128)(2,1)} %copy.27), calls=%async_computation.1 | async-start | bytes 6422528 | tf_op jit(solution)/shard_map/all_to_all | solution.py:19
  70.7 68.7 %all-gather.3.cloned.1.call-start = ((), (), s32[]{:S(2)}) async-start(), calls=%async_computation.4 | async-start | bytes 1705984 | tf_op jit(solution)/shard_map/all_gather | solution.py:27
  71.4 325.4 %all-reduce.2.cloned.1.call-start = ((), (), s32[]{:S(2)}) async-start(), calls=%async_computation.3 | async-start | bytes 5734400 | tf_op jit(solution)/shard_map/psum | solution.py:26
  112.6 4.3 copy-start
  112.6 4.3 copy-start.1
  112.6 4.3 copy-start.4
  129.0 0.7 copy-start.3
  129.0 0.7 copy-start.5
Sparse Core Ops, SparseCore 0:
  74.2 65.0 all-gather.2
Sparse Core Ops, SparseCore 1:
  129.1 267.7 all-reduce.1
where the time goes:
time: 517 us; the launch traced here: 516 us
  waiting for transfers between devices  339 us (66%)
  blocking collectives  73.9 us (14%)
  local copies, waits for them, and re-layouts  45.7 us (9%)
  starting transfers between devices  15.3 us (3%)
  between operations  14.9 us (3%)
  other arithmetic  14.3 us (3%)
  matrix products  12.9 us (2%)
    psum x1, waiting for transfers between devices, body(): correction = lax.psum(partial_value, ('grp', 'ing'))  254 us
    all_to_all x1, blocking collectives, body(): lax.all_to_all(scaled, 'ing', split_axis=1, concat_axis=0, tiled=True)  73.9 us
    all_to_all x1, waiting for transfers between devices, body(): lax.all_to_all(amplitudes, 'ing', split_axis=0, concat_axis=1, tiled=True)  39.1 us
    all_to_all x1, waiting for transfers between devices, body(): lax.all_to_all(integrals, 'ing', split_axis=0, concat_axis=1, tiled=True)  35.5 us
    all_to_all x2, local copies, waits for them, and re-layouts, body(): lax.all_to_all(scaled, 'ing', split_axis=1, concat_axis=0, tiled=True)  13.5 us
  transfers between devices with their start and end apart: 4, of which 4 were waited for; matrix products, arithmetic and copies ran while one was open for 6% of the time, Pallas kernels for 0%

commit v1 on v0

--- a/solution.py
+++ b/solution.py
@@ -2,6 +2,17 @@
 import jax.numpy as jnp
 from jax import lax
 from jax.sharding import PartitionSpec as P
+
+
+def compute_spot(content, array_axis, local):
+    state_next, wide_out = (content.shape[:array_axis], content.shape[array_axis + 1 :])
+    return jnp.moveaxis(content.reshape(*state_next, local, -1, *wide_out), array_axis, 0)
+
+
+def rest_series(inp, at_axis):
+    val = list(inp.shape[1:])
+    val[at_axis] *= inp.shape[0]
+    return jnp.moveaxis(inp, 0, at_axis).reshape(val)
 
 
 def symmetry_mask(values, pair_irrep, virtual_irrep):
@@ -14,9 +25,20 @@
 
 def body(amplitudes, integrals, fock_block, virtual_irrep, pair_irrep, pair_energy, virtual_energy):
     same_irrep = virtual_irrep[:, None] == virtual_irrep[None, :]
+
+    def plan_the_cycles(local_x, across, z, z_in):
+        before, finding = (lax.axis_size(across), lax.axis_index(across))
+        plain = compute_spot(local_x, z, before)
+        pieces_in = [plain[finding]]
+        for num in range(1, before):
+            r2 = plain[finding ^ num]
+            pieces_in.append(lax.ppermute(r2, across, [(h, h ^ num) for h in range(before)]))
+        plain = jnp.stack(pieces_in)[finding ^ jnp.arange(before)]
+        return rest_series(plain, z_in)
+
     whole_amps, whole_ints = (
         lax.all_to_all(amplitudes, "ing", split_axis=0, concat_axis=1, tiled=True),
-        lax.all_to_all(integrals, "ing", split_axis=0, concat_axis=1, tiled=True),
+        plan_the_cycles(integrals, "ing", 0, 1),
     )
     amp_masked = symmetry_mask(whole_amps, pair_irrep, virtual_irrep)
     int_masked = symmetry_mask(whole_ints, pair_irrep, virtual_irrep)

time: 517 us -> 541 us (1.046); the launches traced: 516 us -> 532 us
  waiting for transfers between devices: 339 us -> 302 us
  starting transfers between devices: 15.3 us -> 46.4 us
  local copies, waits for them, and re-layouts: 45.7 us -> 67.3 us
    all_to_all x1, waiting for transfers between devices: 39.1 us -> 0.01 us  [body(): lax.all_to_all(amplitudes, 'ing', split_axis=0, concat_axis=1, tiled=True)]
    ppermute x0 -> x15, starting transfers between devices: none -> 38.6 us  [plan_the_cycles(): lax.ppermute(r2, across, [(h, h ^ num) for h in range(before)])]
    all_to_all x1 -> x0, waiting for transfers between devices: 35.5 us -> none  [body(): lax.all_to_all(integrals, 'ing', split_axis=0, concat_axis=1, tiled=True)]
    ppermute x0 -> x15, waiting for transfers between devices: none -> 28.2 us  [plan_the_cycles(): lax.ppermute(r2, across, [(h, h ^ num) for h in range(before)])]
    psum x1, waiting for transfers between devices: 254 us -> 273 us  [body(): correction = lax.psum(partial_value, ('grp', 'ing'))]
    all_gather x1, waiting for transfers between devices: 9.61 us -> 0.01 us  [body(): fock_full = lax.all_gather(fock_block, 'ing', axis=0, tiled=True)]
    gather x0 -> x1, local copies, waits for them, and re-layouts: none -> 8.84 us  [plan_the_cycles(): plain = jnp.stack(pieces_in)[finding ^ jnp.arange(before)]]
    all_to_all x1 -> x0, starting transfers between devices: 8.32 us -> none  [body(): lax.all_to_all(integrals, 'ing', split_axis=0, concat_axis=1, tiled=True)]
  transfers between devices with their start and end apart: 4 -> 18, of which waited for: 4 -> 4; matrix products, arithmetic and copies ran while one was open for 6% -> 8% of each run, Pallas kernels for 0% -> 0%
where the time goes in v1:
time: 541 us; the launch traced here: 532 us
  waiting for transfers between devices  302 us (56%)
  blocking collectives  73.9 us (14%)
  local copies, waits for them, and re-layouts  67.3 us (12%)
  starting transfers between devices  46.4 us (9%)
  between operations  15.5 us (3%)
  other arithmetic  14.1 us (3%)
  matrix products  12.8 us (2%)
    psum x1, waiting for transfers between devices, body(): correction = lax.psum(partial_value, ('grp', 'ing'))  273 us
    all_to_all x1, blocking collectives, body(): lax.all_to_all(scaled, 'ing', split_axis=1, concat_axis=0, tiled=True)  73.9 us
    ppermute x15, starting transfers between devices, plan_the_cycles(): lax.ppermute(r2, across, [(h, h ^ num) for h in range(before)])  38.6 us
    ppermute x15, waiting for transfers between devices, plan_the_cycles(): lax.ppermute(r2, across, [(h, h ^ num) for h in range(before)])  28.2 us
    unnamed x45, local copies, waits for them, and re-layouts  16.4 us
    all_to_all x2, local copies, waits for them, and re-layouts, body(): lax.all_to_all(scaled, 'ing', split_axis=1, concat_axis=0, tiled=True)  13.5 us
  transfers between devices with their start and end apart: 18, of which 4 were waited for; matrix products, arithmetic and copies ran while one was open for 8% of the time, Pallas kernels for 0%

profile of v1, /device:TPU:99, one launch (start us, length us, event | category | flops | bytes accessed | tf_op | source)
XLA Modules:
  0.0 531.9 jit_solution(3471019632725271473)
XLA Ops:
  7.4 5.7 %reshape.83 = bf16[16,2,50,800]{3,1,0,2:T(2,128)(2,1)S(1)} reshape(bf16[32,50,800]{2,0,1:T(8,128)(2,1)} %param.8) | data formatting | bytes 5120000 | tf_op jit(solution)/shard_map/reshape | solution.py:9
  13.1 0.0 copy-start.3
  13.1 3.1 dynamic-slice_bitcast_fusion
  16.2 0.3 collective-permute-start
  16.5 2.1 collective-permute-start.1
  18.6 0.3 collective-permute-start.2
  18.9 1.3 collective-permute-start.3
  20.2 1.4 collective-permute-start.4
  21.5 2.7 copy.23
  24.2 7.7 %all-to-all-start = ((bf16[32,50,800]{2,1,0:T(8,128)(2,1)}), bf16[32,50,800]{2,1,0:T(8,128)(2,1)}, u32[]{:S(2)}, u32[]{:S(2)}) async-start(bf16[32,50,800]{2,1,0:T(8,128)(2,1)} %copy.23), calls=%async_computation | async-start | bytes 6422528 | tf_op jit(solution)/shard_map/all_to_all | solution.py:40
  32.0 0.0 all-gather.3.cloned.1.call-start
  32.0 0.7 all-gather.3.cloned.1.call-update
  32.7 0.0 all-reduce.2.cloned.1.call-start
  32.7 1.8 broadcast_xor_fusion
  34.6 2.8 collective-permute-start.5
  37.4 0.8 bitcast_dynamic-update-slice_fusion.14
  38.2 0.0 collective-permute-done.1
  38.2 0.8 bitcast_dynamic-update-slice_fusion.13
  39.0 2.4 collective-permute-start.7
  41.4 0.8 bitcast_dynamic-update-slice_fusion.12
  42.3 0.0 collective-permute-done.3
  42.3 2.4 collective-permute-start.8
  44.6 0.8 bitcast_dynamic-update-slice_fusion.11
  45.4 0.0 collective-permute-done.4
  45.4 3.0 collective-permute-start.9
  48.4 0.8 bitcast_dynamic-update-slice_fusion.10
  49.2 24.7 %collective-permute-done.5 = bf16[2,50,800]{2,0,1:T(2,128)(2,1)S(1)} collective-permute-done((bf16[2,50,800]{2,0,1:T(2,128)(2,1)S(1)}, bf16[2,50,800]{2,0,1:T(2,128)(2,1)S(1)}, u32[]{:S(2)}, u32[]{:S(2)}) %collective-permute-start.5) | collective-permute-done | bytes 160032 | tf_op jit(solution)/shard_map/ppermute | solution.py:35
  74.0 14.3 %collective-permute-start.10 = (bf16[2,50,800]{2,0,1:T(2,128)(2,1)S(1)}, bf16[2,50,800]{2,0,1:T(2,128)(2,1)S(1)}, u32[]{:S(2)}, u32[]{:S(2)}) collective-permute-start(bf16[2,50,800]{2,0,1:T(2,128)(2,1)S(1)} %copy-done.5), channel_id=1, source_target_pairs={{0,11},{1,10},{2,9},{3,8},{4,15},{5,14},{6,13},{7,12},{8,3},{9,2},... | collective-permute-start | bytes 480008 | tf_op jit(solution)/shard_map/ppermute | solution.py:35
  88.3 0.8 bitcast_dynamic-update-slice_fusion.9
  89.2 0.1 collective-permute-start.11
  89.3 0.8 bitcast_dynamic-update-slice_fusion.8
  90.1 0.0 collective-permute-done.7
  90.1 5.0 collective-permute-start.12
  95.1 0.8 bitcast_dynamic-update-slice_fusion.7
  95.9 2.4 collective-permute-start.13
  98.3 0.8 bitcast_dynamic-update-slice_fusion.6
  99.1 1.0 collective-permute-start.14
  100.0 0.8 bitcast_dynamic-update-slice_fusion.5
  100.9 0.8 bitcast_dynamic-update-slice_fusion.4
  101.7 0.8 bitcast_dynamic-update-slice_fusion.3
  102.5 0.8 bitcast_dynamic-update-slice_fusion.2
  103.3 0.9 collective-permute-done.13
  104.3 0.8 bitcast_dynamic-update-slice_fusion.1
  105.1 2.5 collective-permute-done.14
  107.6 0.8 bitcast_dynamic-update-slice_fusion
  108.4 8.8 %gather_fusion = bf16[16,2,50,800]{3,1,2,0:T(2,128)(2,1)S(1)} fusion(bf16[16,2,50,800]{3,1,0,2:T(2,128)(2,1)} %bitcast_dynamic-update-slice_fusion, s32[1024]{0:T(1024)S(1)} %pad_clamp_fusion), kind=kCustom, calls=%fused_computation | custom fusion | bytes 5120064 | tf_op jit(solution)/shard_map/gather | solution.py:36
  117.3 0.0 copy-start.13
  117.3 4.3 copy.24
  121.6 7.1 %compare_select_fusion = (bf16[2,800,800]{2,0,1:T(2,128)(2,1)S(1)}, bf16[2,800,800]{2,0,1:T(2,128)(2,1)S(1)}) fusion(bf16[16,2,50,800]{3,1,2,0:T(2,128)(2,1)S(1)} %gather_fusion, s32[800,800]{1,0:T(8,128)S(1)} %copy-done, s32[2]{0:T(128)S(1)} %copy-done.13, bf16[16,2,50,800]{3,1,2,0:T(2,128)(2,1)S(1)} %copy.24), kind=kLoop, calls=%fused_computation.1 | loop fusion | flops 3840000 | bytes 12800008 | tf_op jit(solution)/shard_map/jit(_where)/select_n | solution.py:23
  128.7 0.0 copy-start.1
  128.7 1.6 copy-done.1
  130.3 4.7 fusion.6
  135.0 0.0 all-reduce.2.cloned.1.call-update
  135.1 0.7 copy-done.12
  135.7 0.1 broadcast_subtract_fusion
  135.8 3.2 reshape.95
  139.0 273.0 %all-reduce.2.cloned.1.call-done = f32[800,800]{1,0:T(8,128)} async-done(((f32[800,800]{1,0:T(8,128)}), f32[800,800]{1,0:T(8,128)}) %all-reduce.2.cloned.1.call-update) | async-done | bytes 2560016 | tf_op jit(solution)/shard_map/psum | solution.py:48
  411.9 8.1 %fusion.4 = f32[2,800,800]{2,1,0:T(8,128)} fusion(bf16[2,800,800]{2,0,1:T(2,128)(2,1)S(1)} %copy-done.2, f32[800,800]{1,0:T(8,128)} %all-reduce.2.cloned.1.call-done, f32[800,800]{1,0:T(8,128)} %reshape.95, s32[800]{0:T(1024)S(1)} %copy-done.11), kind=kOutput, calls=%fused_computation.9 | convolution fusion | flops 2050560000 | bytes 12803200 | tf_op jit(solution)/shard_map/pae,be->pab/dot_general | solution.py:54
  420.0 7.1 %copy.28 = f32[2,800,800]{1,2,0:T(8,128)} copy(f32[2,800,800]{2,1,0:T(8,128)} %fusion.4) | data formatting | bytes 10240000 | tf_op jit(solution)/shard_map/pae,be->pab/dot_general | solution.py:54
  427.1 5.1 fusion
  432.2 4.4 copy.29
  436.6 73.9 %all_to_all.36 = f32[2,800,800]{2,0,1:T(2,128)S(1)} all-to-all(f32[2,800,800]{2,0,1:T(2,128)S(1)} %copy.29), channel_id=1, replica_groups=mesh['grp'=16,'ing'=16] {'ing'}, dimensions={1} | all-to-all | bytes 10240000 | tf_op jit(solution)/shard_map/all_to_all | solution.py:59
  510.5 5.7 %copy.30 = f32[16,2,50,800]{3,1,0,2:T(2,128)} copy(f32[16,2,50,800]{3,1,2,0:T(2,128)S(1)} %bitcast.88) | data formatting | bytes 10240000 | tf_op jit(solution)/shard_map/all_to_all | solution.py:59
  516.2 7.8 %all_to_all.33 = f32[32,50,800]{2,0,1:T(8,128)} reshape(f32[16,2,50,800]{3,1,0,2:T(2,128)} %copy.30) | data formatting | bytes 10240000 | tf_op jit(solution)/shard_map/all_to_all | solution.py:59
  (38 shorter events, 0.1 us)
Async XLA Ops:
  13.1 8.4 %copy-start.3 = (bf16[32,50,800]{2,0,1:T(8,128)(2,1)S(1)}, bf16[32,50,800]{2,0,1:T(8,128)(2,1)}, u32[]{:S(2)}) copy-start(bf16[32,50,800]{2,0,1:T(8,128)(2,1)} %param.7) | copy-start | bytes 7680004
  16.2 18.4 %collective-permute-start = (bf16[2,50,800]{2,0,1:T(2,128)(2,1)}, bf16[2,50,800]{2,0,1:T(2,128)(2,1)S(1)}, u32[]{:S(2)}, u32[]{:S(2)}) collective-permute-start(bf16[2,50,800]{2,0,1:T(2,128)(2,1)} %get-tuple-element.21), channel_id=1, source_target_pairs={{0,1},{1,0},{2,3},{3,2},{4,5},{5,4},{6,7},{7,6},{8,9},{9,8},{10,11... | collective-permute-start | bytes 480008 | tf_op jit(solution)/shard_map/ppermute | solution.py:35
  16.5 21.7 %collective-permute-start.1 = (bf16[2,50,800]{2,0,1:T(2,128)(2,1)}, bf16[2,50,800]{2,0,1:T(2,128)(2,1)S(1)}, u32[]{:S(2)}, u32[]{:S(2)}) collective-permute-start(bf16[2,50,800]{2,0,1:T(2,128)(2,1)} %get-tuple-element.20), channel_id=1, source_target_pairs={{0,2},{1,3},{2,0},{3,1},{4,6},{5,7},{6,4},{7,5},{8,10},{9,11},{10,... | collective-permute-start | bytes 480008 | tf_op jit(solution)/shard_map/ppermute | solution.py:35
  18.6 20.4 %collective-permute-start.2 = (bf16[2,50,800]{2,0,1:T(2,128)(2,1)}, bf16[2,50,800]{2,0,1:T(2,128)(2,1)S(1)}, u32[]{:S(2)}, u32[]{:S(2)}) collective-permute-start(bf16[2,50,800]{2,0,1:T(2,128)(2,1)} %get-tuple-element.19), channel_id=1, source_target_pairs={{0,3},{1,2},{2,1},{3,0},{4,7},{5,6},{6,5},{7,4},{8,11},{9,10},{10,... | collective-permute-start | bytes 480008 | tf_op jit(solution)/shard_map/ppermute | solution.py:35
  18.9 23.4 %collective-permute-start.3 = (bf16[2,50,800]{2,0,1:T(2,128)(2,1)}, bf16[2,50,800]{2,0,1:T(2,128)(2,1)S(1)}, u32[]{:S(2)}, u32[]{:S(2)}) collective-permute-start(bf16[2,50,800]{2,0,1:T(2,128)(2,1)} %get-tuple-element.18), channel_id=1, source_target_pairs={{0,4},{1,5},{2,6},{3,7},{4,0},{5,1},{6,2},{7,3},{8,12},{9,13},{10,... | collective-permute-start | bytes 480008 | tf_op jit(solution)/shard_map/ppermute | solution.py:35
  20.2 25.3 %collective-permute-start.4 = (bf16[2,50,800]{2,0,1:T(2,128)(2,1)}, bf16[2,50,800]{2,0,1:T(2,128)(2,1)S(1)}, u32[]{:S(2)}, u32[]{:S(2)}) collective-permute-start(bf16[2,50,800]{2,0,1:T(2,128)(2,1)} %get-tuple-element.17), channel_id=1, source_target_pairs={{0,5},{1,4},{2,7},{3,6},{4,1},{5,0},{6,3},{7,2},{8,13},{9,12},{10,... | collective-permute-start | bytes 480008 | tf_op jit(solution)/shard_map/ppermute | solution.py:35
  24.2 8.6 %copy-start.11 = (s32[800]{0:T(1024)S(1)}, s32[800]{0:T(1024)}, u32[]{:S(2)}) copy-start(s32[800]{0:T(1024)} %param.10) | copy-start | bytes 9604
  24.2 93.1 %all-to-all-start = ((bf16[32,50,800]{2,1,0:T(8,128)(2,1)}), bf16[32,50,800]{2,1,0:T(8,128)(2,1)}, u32[]{:S(2)}, u32[]{:S(2)}) async-start(bf16[32,50,800]{2,1,0:T(8,128)(2,1)} %copy.23), calls=%async_computation | async-start | bytes 6422528 | tf_op jit(solution)/shard_map/all_to_all | solution.py:40
  31.9 2.7 copy-start.10
  31.9 6.3 %copy-start.9 = (bf16[2,50,800]{2,0,1:T(2,128)(2,1)S(1)}, bf16[2,50,800]{2,0,1:T(2,128)(2,1)}, u32[]{:S(2)}) copy-start(bf16[2,50,800]{2,0,1:T(2,128)(2,1)} %get-tuple-element.15) | copy-start | bytes 480004
  31.9 7.1 %copy-start.8 = (bf16[2,50,800]{2,0,1:T(2,128)(2,1)S(1)}, bf16[2,50,800]{2,0,1:T(2,128)(2,1)}, u32[]{:S(2)}) copy-start(bf16[2,50,800]{2,0,1:T(2,128)(2,1)} %get-tuple-element.14) | copy-start | bytes 480004
  31.9 10.4 %copy-start.7 = (bf16[2,50,800]{2,0,1:T(2,128)(2,1)S(1)}, bf16[2,50,800]{2,0,1:T(2,128)(2,1)}, u32[]{:S(2)}) copy-start(bf16[2,50,800]{2,0,1:T(2,128)(2,1)} %get-tuple-element.13) | copy-start | bytes 480004
  31.9 13.5 %copy-start.6 = (bf16[2,50,800]{2,0,1:T(2,128)(2,1)S(1)}, bf16[2,50,800]{2,0,1:T(2,128)(2,1)}, u32[]{:S(2)}) copy-start(bf16[2,50,800]{2,0,1:T(2,128)(2,1)} %get-tuple-element.12) | copy-start | bytes 480004
  31.9 42.0 %copy-start.5 = (bf16[2,50,800]{2,0,1:T(2,128)(2,1)S(1)}, bf16[2,50,800]{2,0,1:T(2,128)(2,1)}, u32[]{:S(2)}) copy-start(bf16[2,50,800]{2,0,1:T(2,128)(2,1)} %get-tuple-element.11) | copy-start | bytes 480004
  31.9 57.2 %copy-start.4 = (bf16[2,50,800]{2,0,1:T(2,128)(2,1)S(1)}, bf16[2,50,800]{2,0,1:T(2,128)(2,1)}, u32[]{:S(2)}) copy-start(bf16[2,50,800]{2,0,1:T(2,128)(2,1)} %get-tuple-element.10) | copy-start | bytes 480004
  32.0 103.8 %all-gather.3.cloned.1.call-start = ((), (), s32[]{:S(2)}) async-start(), calls=%async_computation.3 | async-start | bytes 1705984 | tf_op jit(solution)/shard_map/all_gather | solution.py:49
  32.7 379.2 %all-reduce.2.cloned.1.call-start = ((), (), s32[]{:S(2)}) async-start(), calls=%async_computation.2 | async-start | bytes 5734400 | tf_op jit(solution)/shard_map/psum | solution.py:48
  34.6 39.4 %collective-permute-start.5 = (bf16[2,50,800]{2,0,1:T(2,128)(2,1)S(1)}, bf16[2,50,800]{2,0,1:T(2,128)(2,1)S(1)}, u32[]{:S(2)}, u32[]{:S(2)}) collective-permute-start(bf16[2,50,800]{2,0,1:T(2,128)(2,1)S(1)} %copy-done.10), channel_id=1, source_target_pairs={{0,6},{1,7},{2,4},{3,5},{4,2},{5,3},{6,0},{7,1},{8,14},{9,15},{10,... | collective-permute-start | bytes 480008 | tf_op jit(solution)/shard_map/ppermute | solution.py:35
  38.2 50.9 %collective-permute-start.6 = (bf16[2,50,800]{2,0,1:T(2,128)(2,1)S(1)}, bf16[2,50,800]{2,0,1:T(2,128)(2,1)S(1)}, u32[]{:S(2)}, u32[]{:S(2)}) collective-permute-start(bf16[2,50,800]{2,0,1:T(2,128)(2,1)S(1)} %copy-done.9), channel_id=1, source_target_pairs={{0,7},{1,6},{2,5},{3,4},{4,3},{5,2},{6,1},{7,0},{8,15},{9,14},{10,... | collective-permute-start | bytes 480008 | tf_op jit(solution)/shard_map/ppermute | solution.py:35
  39.0 51.1 %collective-permute-start.7 = (bf16[2,50,800]{2,0,1:T(2,128)(2,1)S(1)}, bf16[2,50,800]{2,0,1:T(2,128)(2,1)S(1)}, u32[]{:S(2)}, u32[]{:S(2)}) collective-permute-start(bf16[2,50,800]{2,0,1:T(2,128)(2,1)S(1)} %copy-done.8), channel_id=1, source_target_pairs={{0,8},{1,9},{2,10},{3,11},{4,12},{5,13},{6,14},{7,15},{8,0},{9,1},... | collective-permute-start | bytes 480008 | tf_op jit(solution)/shard_map/ppermute | solution.py:35
  42.3 53.6 %collective-permute-start.8 = (bf16[2,50,800]{2,0,1:T(2,128)(2,1)S(1)}, bf16[2,50,800]{2,0,1:T(2,128)(2,1)S(1)}, u32[]{:S(2)}, u32[]{:S(2)}) collective-permute-start(bf16[2,50,800]{2,0,1:T(2,128)(2,1)S(1)} %copy-done.7), channel_id=1, source_target_pairs={{0,9},{1,8},{2,11},{3,10},{4,13},{5,12},{6,15},{7,14},{8,1},{9,0},... | collective-permute-start | bytes 480008 | tf_op jit(solution)/shard_map/ppermute | solution.py:35
  45.4 53.6 %collective-permute-start.9 = (bf16[2,50,800]{2,0,1:T(2,128)(2,1)S(1)}, bf16[2,50,800]{2,0,1:T(2,128)(2,1)S(1)}, u32[]{:S(2)}, u32[]{:S(2)}) collective-permute-start(bf16[2,50,800]{2,0,1:T(2,128)(2,1)S(1)} %copy-done.6), channel_id=1, source_target_pairs={{0,10},{1,11},{2,8},{3,9},{4,14},{5,15},{6,12},{7,13},{8,2},{9,3},... | collective-permute-start | bytes 480008 | tf_op jit(solution)/shard_map/ppermute | solution.py:35
  74.0 26.9 %collective-permute-start.10 = (bf16[2,50,800]{2,0,1:T(2,128)(2,1)S(1)}, bf16[2,50,800]{2,0,1:T(2,128)(2,1)S(1)}, u32[]{:S(2)}, u32[]{:S(2)}) collective-permute-start(bf16[2,50,800]{2,0,1:T(2,128)(2,1)S(1)} %copy-done.5), channel_id=1, source_target_pairs={{0,11},{1,10},{2,9},{3,8},{4,15},{5,14},{6,13},{7,12},{8,3},{9,2},... | collective-permute-start | bytes 480008 | tf_op jit(solution)/shard_map/ppermute | solution.py:35
  89.2 12.6 %collective-permute-start.11 = (bf16[2,50,800]{2,0,1:T(2,128)(2,1)S(1)}, bf16[2,50,800]{2,0,1:T(2,128)(2,1)S(1)}, u32[]{:S(2)}, u32[]{:S(2)}) collective-permute-start(bf16[2,50,800]{2,0,1:T(2,128)(2,1)S(1)} %copy-done.4), channel_id=1, source_target_pairs={{0,12},{1,13},{2,14},{3,15},{4,8},{5,9},{6,10},{7,11},{8,4},{9,5},... | collective-permute-start | bytes 480008 | tf_op jit(solution)/shard_map/ppermute | solution.py:35
  90.1 12.4 %collective-permute-start.12 = (bf16[2,50,800]{2,0,1:T(2,128)(2,1)S(1)}, bf16[2,50,800]{2,0,1:T(2,128)(2,1)S(1)}, u32[]{:S(2)}, u32[]{:S(2)}) collective-permute-start(bf16[2,50,800]{2,0,1:T(2,128)(2,1)S(1)} %get-tuple-element.9), channel_id=1, source_target_pairs={{0,13},{1,12},{2,15},{3,14},{4,9},{5,8},{6,11},{7,10},{8,5},{9,4},... | collective-permute-start | bytes 480008 | tf_op jit(solution)/shard_map/ppermute | solution.py:35
  95.9 8.3 %collective-permute-start.13 = (bf16[2,50,800]{2,0,1:T(2,128)(2,1)S(1)}, bf16[2,50,800]{2,0,1:T(2,128)(2,1)S(1)}, u32[]{:S(2)}, u32[]{:S(2)}) collective-permute-start(bf16[2,50,800]{2,0,1:T(2,128)(2,1)S(1)} %get-tuple-element.8), channel_id=1, source_target_pairs={{0,14},{1,15},{2,12},{3,13},{4,10},{5,11},{6,8},{7,9},{8,6},{9,7},... | collective-permute-start | bytes 480008 | tf_op jit(solution)/shard_map/ppermute | solution.py:35
  99.1 8.5 %collective-permute-start.14 = (bf16[2,50,800]{2,0,1:T(2,128)(2,1)S(1)}, bf16[2,50,800]{2,0,1:T(2,128)(2,1)S(1)}, u32[]{:S(2)}, u32[]{:S(2)}) collective-permute-start(bf16[2,50,800]{2,0,1:T(2,128)(2,1)S(1)} %get-tuple-element.7), channel_id=1, source_target_pairs={{0,15},{1,14},{2,13},{3,12},{4,11},{5,10},{6,9},{7,8},{8,7},{9,6},... | collective-permute-start | bytes 480008 | tf_op jit(solution)/shard_map/ppermute | solution.py:35
  117.3 4.3 copy-start
  117.3 4.3 copy-start.13
  128.7 1.6 copy-start.1
  135.0 0.7 copy-start.12
  135.0 0.7 copy-start.14
  135.7 276.2 %copy-start.2 = (bf16[2,800,800]{2,0,1:T(2,128)(2,1)S(1)}, bf16[2,800,800]{2,0,1:T(2,128)(2,1)}, u32[]{:S(2)}) copy-start(bf16[2,800,800]{2,0,1:T(2,128)(2,1)} %copy-done.1) | copy-start | bytes 7680004
Sparse Core Ops, SparseCore 0:
  35.5 87.8 all-gather.2
Sparse Core Ops, SparseCore 1:
  135.1 276.7 all-reduce.1
